TPU v7x, 256 devices: a whole 4x4x8 slice. The times are simulated.
256 devices in a mesh: node: 64 (over z, y, core), state: 4 (over x).
Axes of the slice: x: 4, y: 4, z: 8, core: 2. Of those that a mesh axis runs over, the one named last changes fastest.
Arguments:
- block: bfloat16 [64, 2097152], P('state', 'node'), may hold values from -6 to 6
- connectivity: int32 [125, 32768], P(None, 'node'), may hold values from 0 to 49151, as said below
- potential: float32 [125, 32768], P(None, 'node'), may hold values from 0.1 to 3
- cell_matrix: bfloat16 [125, 125], replicated, as said below
Outputs:
- orthonormal: bfloat16 [64, 2097152], P('state', 'node')
- factor: float32 [64, 64], replicated
Inputs may be any that keep to these rules, and one draw needn't show every extreme that they name: `connectivity`: in each slab, numbers below 8192 are the previous slab's last 8192 nodes and numbers from 40960 on are the next slab's first nodes. The numbers of the slab's k-th cell (k from 0) lie in k * 96 to k * 96 + 2 * 96 - 1, those of its last cell in k * 96 to k * 96 + 95; each cell reaches the lower end of its range. `cell_matrix`: Symmetric.
All inputs are finite; a program needn't handle non-finite values.
Results may differ from a plain program's by a relative error of at most 0.015.
Values may be sent and summed in bfloat16 or wider, within the bound.
No kernel may reach another device: no remote copies, remote signals or barrier semaphores. Data moves between devices by JAX's collectives and lax.ppermute only.
A program may use at most 64 MiB of HBM per device.

v0:
```python
import jax
import jax.numpy as jnp
from jax import lax
from jax.sharding import PartitionSpec as P

CENTER = 3.0
HALF_WIDTH = 3.0


def extended(block, sides, width):
    for axis, dim in sides:
        count = lax.axis_size(axis)
        forward = [(i, i + 1) for i in range(count - 1)]
        backward = [(target, source) for source, target in forward]
        low = lax.ppermute(
            lax.slice_in_dim(block, block.shape[dim] - width, None, axis=dim), axis, forward
        )
        high = lax.ppermute(lax.slice_in_dim(block, 0, width, axis=dim), axis, backward)
        block = jnp.concatenate([low, block, high], axis=dim)
    return block


def passed_along(block, axis, distance):
    devices = range(lax.axis_size(axis))
    route = [(i - distance, i) for i in devices if i - distance in devices]
    return lax.ppermute(block, axis, route)


def cell_terms(window, connectivity, potential, cell_matrix):
    states = window.shape[0]
    cells = connectivity.shape[1]
    stride = window.shape[1] // cells
    segments = window.reshape(states, cells, stride)
    following = jnp.concatenate(
        [segments[:, 1:], jnp.zeros((states, 1, stride), segments.dtype)], axis=1
    )
    paired = jnp.concatenate([segments, following], axis=2)
    offsets = jnp.arange(cells, dtype=jnp.int32) * stride
    local_links = connectivity - offsets[None, :]
    columns = jnp.arange(2 * stride, dtype=jnp.int32)
    group = min(cells, 128)
    pieces = []
    for first_cell in range(0, cells, group):
        links = local_links[:, first_cell : first_cell + group]
        picker = links[:, :, None] == columns[None, None, :]
        picker_half = picker.astype(jnp.bfloat16)
        part_pair = paired[:, first_cell : first_cell + group]
        values = jnp.einsum(
            "skn,jkn->sjk", part_pair, picker_half, preferred_element_type=jnp.float32
        )
        mixed = jnp.einsum(
            "ij,sjk->sik",
            cell_matrix,
            values.astype(jnp.bfloat16),
            preferred_element_type=jnp.float32,
        )
        mixed = mixed + potential[None, :, first_cell : first_cell + group] * values
        spread = jnp.einsum(
            "sjk,jkn->skn", mixed, picker.astype(jnp.float32), precision=lax.Precision.HIGHEST
        )
        pieces.append(spread)
    spread = jnp.concatenate(pieces, axis=1)
    lower = spread[:, :, :stride]
    upper = spread[:, :, stride:]
    shifted = jnp.concatenate([jnp.zeros((states, 1, stride), jnp.float32), upper[:, :-1]], axis=1)
    return (lower + shifted).reshape(states, cells * stride)


def operate(field, connectivity, potential, cell_matrix):
    owned = field.shape[1]
    margin = owned // 4
    window = extended(field, (("node", 1),), margin)
    summed = cell_terms(window, connectivity, potential, cell_matrix)
    result = summed[:, margin : margin + owned]
    from_above = passed_along(summed[:, :margin].astype(jnp.bfloat16), "node", -1).astype(
        jnp.float32
    )
    from_below = passed_along(summed[:, margin + owned :].astype(jnp.bfloat16), "node", 1).astype(
        jnp.float32
    )
    result = result.at[:, owned - margin :].add(from_above)
    result = result.at[:, :margin].add(from_below)
    return result


def factorize(intersection):
    factor = jnp.linalg.cholesky(intersection)
    identity = jnp.eye(intersection.shape[0], dtype=factor.dtype)
    inverse = lax.linalg.triangular_solve(factor, identity, left_side=True, lower=True).astype(
        jnp.bfloat16
    )
    return (factor, inverse)


def per_device(block, connectivity, potential, cell_matrix):
    start = block.astype(jnp.float32)
    image = operate(block, connectivity, potential, cell_matrix)
    first = ((image - CENTER * start) / HALF_WIDTH).astype(jnp.bfloat16)
    image = operate(first, connectivity, potential, cell_matrix)
    second = (2.0 * (image - CENTER * first.astype(jnp.float32)) / HALF_WIDTH - start).astype(
        jnp.bfloat16
    )
    total_nodes = block.shape[1] * lax.axis_size("node")
    panel = lax.all_gather(second, "state", axis=0, tiled=True)
    partial_intersection = jnp.einsum("an,bn->ab", panel, panel, preferred_element_type=jnp.float32)
    intersection = lax.psum(partial_intersection, "node") / total_nodes
    factor, inverse = factorize(intersection)
    rows = second.shape[0]
    mine = lax.dynamic_slice_in_dim(inverse, lax.axis_index("state") * rows, rows, 0)
    orthonormal = jnp.dot(mine, panel, preferred_element_type=jnp.float32).astype(jnp.bfloat16)
    return (orthonormal, factor)


def solution(mesh):
    return jax.shard_map(
        per_device,
        mesh=mesh,
        in_specs=(P("state", "node"), P(None, "node"), P(None, "node"), P()),
        out_specs=(P("state", "node"), P()),
        check_vma=False,
    )
```

profile of v0, /device:TPU:2, one launch (start us, length us, event | category | flops | bytes accessed | tf_op | source)
XLA Modules:
  0.0 566.9 jit_solution(16091128970053678684)
XLA Ops:
  8.4 1.8 collective-permute-start
  10.1 1.3 collective-permute-start.1
  16.8 3.2 reshape.132
  20.0 1.4 copy.18
  21.7 2.8 fusion.34
  24.5 3.0 fusion.123
  28.4 4.3 fusion.122
  33.6 4.3 fusion.121
  38.2 1.5 copy.37
  39.8 4.2 fusion.120
  44.3 1.4 copy.39
  45.8 11.6 %fusion.42 = f32[16,128,192]{2,0,1:T(8,128)S(1)} fusion(s32[125,128]{0,1:T(8,128)S(1)} %copy.16, f32[16,128,125]{2,0,1:T(8,128)S(1)} %copy.33, f32[16,125,128]{1,0,2:T(8,128)} %get-tuple-element.75, f32[125,128]{0,1:T(8,128)} %copy.19), kind=kOutput, calls=%fused_computation.59 | convolution fusion | flops 593408000 | bytes 3748864 | tf_op jit(solution)/shard_map/sjk,jkn->skn/dot_general | solution.py:58
  57.4 9.9 %fusion.44 = f32[16,128,192]{2,0,1:T(8,128)S(1)} fusion(s32[125,128]{0,1:T(8,128)S(1)} %copy-done.11, f32[16,128,125]{2,0,1:T(8,128)S(1)} %copy.35, f32[16,125,128]{1,0,2:T(8,128)S(1)} %copy-done.19, f32[125,128]{0,1:T(8,128)S(1)} %copy-done.14), kind=kOutput, calls=%fused_computation.61 | convolution fusion | flops 593408000 | bytes 3748864 | tf_op jit(solution)/shard_map/sjk,jkn->skn/dot_general | solution.py:58
  67.3 10.0 %fusion.46 = f32[16,128,192]{2,0,1:T(8,128)S(1)} fusion(s32[125,128]{0,1:T(8,128)S(1)} %copy.22, f32[16,128,125]{2,0,1:T(8,128)S(1)} %copy-done.7, f32[16,125,128]{1,0,2:T(8,128)S(1)} %copy-done.20, f32[125,128]{0,1:T(8,128)S(1)} %copy.23), kind=kOutput, calls=%fused_computation.63 | convolution fusion | flops 593408000 | bytes 3748864 | tf_op jit(solution)/shard_map/sjk,jkn->skn/dot_general | solution.py:58
  77.3 9.8 %fusion.48 = f32[16,128,192]{2,0,1:T(8,128)S(1)} fusion(s32[125,128]{0,1:T(8,128)S(1)} %copy.24, f32[16,128,125]{2,0,1:T(8,128)S(1)} %copy-done.9, f32[16,125,128]{1,0,2:T(8,128)S(1)} %copy-done.21, f32[125,128]{0,1:T(8,128)S(1)} %copy.25), kind=kOutput, calls=%fused_computation.65 | convolution fusion | flops 593408000 | bytes 3748864 | tf_op jit(solution)/shard_map/sjk,jkn->skn/dot_general | solution.py:58
  88.2 2.3 fusion.37
  90.5 3.2 copy.26
  93.8 4.0 reshape.133
  98.0 1.3 collective-permute-start.2
  100.0 6.8 %collective-permute-start.3 = (bf16[16,8192]{1,0:T(8,128)(2,1)S(1)}, bf16[16,8192]{1,0:T(8,128)(2,1)S(1)}, u32[]{:S(2)}, u32[]{:S(2)}) collective-permute-start(bf16[16,8192]{1,0:T(8,128)(2,1)S(1)} %get-tuple-element.54), channel_id=1, source_target_pairs={{0,4},{4,8},{8,12},{12,16},{16,20},{20,24},{24,28},{28,32},{32,36}... | collective-permute-start | bytes 786440 | tf_op jit(solution)/shard_map/ppermute | solution.py:26
  109.2 5.8 %collective-permute-start.4 = (bf16[16,8192]{1,0:T(8,128)(2,1)S(1)}, bf16[16,8192]{1,0:T(8,128)(2,1)S(1)}, u32[]{:S(2)}, u32[]{:S(2)}) collective-permute-start(bf16[16,8192]{1,0:T(8,128)(2,1)S(1)} %get-tuple-element.56), channel_id=1, source_target_pairs={{0,4},{4,8},{8,12},{12,16},{16,20},{20,24},{24,28},{28,32},{32,36}... | collective-permute-start | bytes 786440 | tf_op jit(solution)/shard_map/ppermute | solution.py:15
  115.0 1.3 collective-permute-start.5
  116.3 4.1 collective-permute-done.5
  121.7 3.2 reshape.134
  124.9 1.4 copy.28
  126.6 3.0 fusion.35
  129.6 3.0 fusion.127
  132.7 3.0 fusion.126
  135.7 3.0 fusion.125
  138.7 3.0 fusion.124
  142.0 1.5 copy.41
  143.8 1.4 copy.43
  147.0 11.7 %fusion.43 = f32[16,128,192]{2,0,1:T(8,128)S(1)} fusion(s32[125,128]{0,1:T(8,128)S(1)} %copy.16, f32[16,128,125]{2,0,1:T(8,128)} %copy.41, f32[16,125,128]{1,0,2:T(8,128)} %get-tuple-element.83, f32[125,128]{0,1:T(8,128)} %copy.19), kind=kOutput, calls=%fused_computation.60 | convolution fusion | flops 593408000 | bytes 3748864 | tf_op jit(solution)/shard_map/sjk,jkn->skn/dot_general | solution.py:58
  158.8 9.9 %fusion.45 = f32[16,128,192]{2,0,1:T(8,128)S(1)} fusion(s32[125,128]{0,1:T(8,128)S(1)} %copy-done.13, f32[16,128,125]{2,0,1:T(8,128)S(1)} %copy-done.8, f32[16,125,128]{1,0,2:T(8,128)S(1)} %copy-done.18, f32[125,128]{0,1:T(8,128)S(1)} %copy-done.15), kind=kOutput, calls=%fused_computation.62 | convolution fusion | flops 593408000 | bytes 3748864 | tf_op jit(solution)/shard_map/sjk,jkn->skn/dot_general | solution.py:58
  168.7 10.0 %fusion.47 = f32[16,128,192]{2,0,1:T(8,128)S(1)} fusion(s32[125,128]{0,1:T(8,128)S(1)} %copy.22, f32[16,128,125]{2,0,1:T(8,128)S(1)} %copy.45, f32[16,125,128]{1,0,2:T(8,128)S(1)} %copy-done.17, f32[125,128]{0,1:T(8,128)S(1)} %copy.23), kind=kOutput, calls=%fused_computation.64 | convolution fusion | flops 593408000 | bytes 3748864 | tf_op jit(solution)/shard_map/sjk,jkn->skn/dot_general | solution.py:58
  178.7 9.8 %fusion.49 = f32[16,128,192]{2,0,1:T(8,128)S(1)} fusion(s32[125,128]{0,1:T(8,128)S(1)} %copy.24, f32[16,128,125]{2,0,1:T(8,128)S(1)} %copy.47, f32[16,125,128]{1,0,2:T(8,128)S(1)} %copy-done.16, f32[125,128]{0,1:T(8,128)S(1)} %copy.25), kind=kOutput, calls=%fused_computation.66 | convolution fusion | flops 593408000 | bytes 3748864 | tf_op jit(solution)/shard_map/sjk,jkn->skn/dot_general | solution.py:58
  189.6 2.3 fusion.36
  192.0 3.2 copy.29
  195.2 4.0 reshape.135
  199.4 1.4 collective-permute-start.6
  201.0 7.3 %collective-permute-start.7 = (bf16[16,8192]{1,0:T(8,128)(2,1)S(1)}, bf16[16,8192]{1,0:T(8,128)(2,1)S(1)}, u32[]{:S(2)}, u32[]{:S(2)}) collective-permute-start(bf16[16,8192]{1,0:T(8,128)(2,1)S(1)} %get-tuple-element.52), channel_id=1, source_target_pairs={{0,4},{4,8},{8,12},{12,16},{16,20},{20,24},{24,28},{28,32},{32,36}... | collective-permute-start | bytes 786440 | tf_op jit(solution)/shard_map/ppermute | solution.py:26
  210.3 1.4 fusion.41
  211.7 75.3 %all-gather.2.cloned.1.call-done = bf16[64,32768]{1,0:T(8,128)(2,1)} async-done(((bf16[16,32768]{1,0:T(8,128)(2,1)}), bf16[64,32768]{1,0:T(8,128)(2,1)}) %all-gather.2.cloned.1.call-update) | async-done | bytes 4194320 | tf_op jit(solution)/shard_map/all_gather | solution.py:104
  287.0 4.7 fusion.128
  291.7 251.0 %psum.7 = f32[64,64]{0,1:T(8,128)S(1)} all-reduce(f32[64,64]{0,1:T(8,128)S(1)} %fusion.128), channel_id=1, replica_groups=mesh['node'=64,'state'=4] {'node'}, use_global_device_ids=true, to_apply=%region_1.0 | all-reduce | flops 4096 | bytes 32768 | tf_op jit(solution)/shard_map/psum | solution.py:106
  542.8 5.8 %cholesky.17 = f32[64,64]{1,0:T(8,128)S(1)} custom-call(f32[64,64]{1,0:T(8,128)S(1)} %fusion.104), custom_call_target="Cholesky" | custom-call | tf_op jit(solution)/shard_map/jit(cholesky)/cholesky | solution.py:87
  550.6 4.9 custom-call.6
  555.8 3.8 convolution_convert_fusion
  (104 shorter events, 23.2 us)
Async XLA Ops:
  7.2 20.4 %copy-start = (bf16[125,125]{1,0:T(8,128)(2,1)S(1)}, bf16[125,125]{1,0:T(8,128)(2,1)}, u32[]{:S(2)}) copy-start(bf16[125,125]{1,0:T(8,128)(2,1)} %param.15) | copy-start | bytes 93754
  7.2 8.4 %copy-start.1 = (bf16[16,32768]{1,0:T(8,128)(2,1)S(1)}, bf16[16,32768]{1,0:T(8,128)(2,1)}, u32[]{:S(2)}) copy-start(bf16[16,32768]{1,0:T(8,128)(2,1)} %param.12) | copy-start | bytes 3145732
  7.2 279.8 %all-gather.2.cloned.1.call-start = ((), (), s32[]{:S(2)}) async-start(), calls=%async_computation | async-start | bytes 5242880 | tf_op jit(solution)/shard_map/all_gather | solution.py:104
  8.4 7.1 %collective-permute-start = (bf16[16,8192]{1,0:T(8,128)(2,1)S(1)}, bf16[16,8192]{1,0:T(8,128)(2,1)S(1)}, u32[]{:S(2)}, u32[]{:S(2)}) collective-permute-start(bf16[16,8192]{1,0:T(8,128)(2,1)S(1)} %get-tuple-element.58), channel_id=1, source_target_pairs={{0,4},{4,8},{8,12},{12,16},{16,20},{20,24},{24,28},{28,32},{32,36}... | collective-permute-start | bytes 786440 | tf_op jit(solution)/shard_map/ppermute | solution.py:15
  10.1 5.4 collective-permute-start.1
  14.4 14.1 %copy-start.10 = (s32[125,128]{0,1:T(8,128)}, s32[125,128]{0,1:T(8,128)S(1)}, u32[]{:S(2)}) copy-start(s32[125,128]{0,1:T(8,128)S(1)} %copy.20) | copy-start | bytes 192004
  24.5 3.0 copy-start.6
  45.8 11.6 %copy-start.11 = (s32[125,128]{0,1:T(8,128)S(1)}, s32[125,128]{0,1:T(8,128)}, u32[]{:S(2)}) copy-start(s32[125,128]{0,1:T(8,128)} %copy-done.10) | copy-start | bytes 192004
  45.8 11.6 %copy-start.14 = (f32[125,128]{0,1:T(8,128)S(1)}, f32[125,128]{0,1:T(8,128)}, u32[]{:S(2)}) copy-start(f32[125,128]{0,1:T(8,128)} %copy.21) | copy-start | bytes 192004
  45.8 11.6 %copy-start.19 = (f32[16,125,128]{1,0,2:T(8,128)S(1)}, f32[16,125,128]{1,0,2:T(8,128)}, u32[]{:S(2)}) copy-start(f32[16,125,128]{1,0,2:T(8,128)} %get-tuple-element.73) | copy-start | bytes 3072004
  57.4 9.9 %copy-start.7 = (f32[16,128,125]{2,0,1:T(8,128)S(1)}, f32[16,128,125]{2,0,1:T(8,128)}, u32[]{:S(2)}) copy-start(f32[16,128,125]{2,0,1:T(8,128)} %copy.37) | copy-start | bytes 3072004
  57.4 9.9 %copy-start.20 = (f32[16,125,128]{1,0,2:T(8,128)S(1)}, f32[16,125,128]{1,0,2:T(8,128)}, u32[]{:S(2)}) copy-start(f32[16,125,128]{1,0,2:T(8,128)} %get-tuple-element.71) | copy-start | bytes 3072004
  67.3 10.0 %copy-start.9 = (f32[16,128,125]{2,0,1:T(8,128)S(1)}, f32[16,128,125]{2,0,1:T(8,128)}, u32[]{:S(2)}) copy-start(f32[16,128,125]{2,0,1:T(8,128)} %copy.39) | copy-start | bytes 3072004
  67.3 10.0 %copy-start.21 = (f32[16,125,128]{1,0,2:T(8,128)S(1)}, f32[16,125,128]{1,0,2:T(8,128)}, u32[]{:S(2)}) copy-start(f32[16,125,128]{1,0,2:T(8,128)} %get-tuple-element.69) | copy-start | bytes 3072004
  98.0 8.9 %collective-permute-start.2 = (bf16[16,8192]{1,0:T(8,128)(2,1)S(1)}, bf16[16,8192]{1,0:T(8,128)(2,1)S(1)}, u32[]{:S(2)}, u32[]{:S(2)}) collective-permute-start(bf16[16,8192]{1,0:T(8,128)(2,1)S(1)} %get-tuple-element.55), channel_id=1, source_target_pairs={{4,0},{8,4},{12,8},{16,12},{20,16},{24,20},{28,24},{32,28},{36,32}... | collective-permute-start | bytes 786440 | tf_op jit(solution)/shard_map/ppermute | solution.py:26
  99.9 8.9 %copy-start.2 = (bf16[16,32768]{1,0:T(8,128)(2,1)S(1)}, bf16[16,32768]{1,0:T(8,128)(2,1)}, u32[]{:S(2)}) copy-start(bf16[16,32768]{1,0:T(8,128)(2,1)} %param.12) | copy-start | bytes 3145732
  100.0 8.0 %collective-permute-start.3 = (bf16[16,8192]{1,0:T(8,128)(2,1)S(1)}, bf16[16,8192]{1,0:T(8,128)(2,1)S(1)}, u32[]{:S(2)}, u32[]{:S(2)}) collective-permute-start(bf16[16,8192]{1,0:T(8,128)(2,1)S(1)} %get-tuple-element.54), channel_id=1, source_target_pairs={{0,4},{4,8},{8,12},{12,16},{16,20},{20,24},{24,28},{28,32},{32,36}... | collective-permute-start | bytes 786440 | tf_op jit(solution)/shard_map/ppermute | solution.py:26
  109.2 11.3 %copy-start.4 = (bf16[16,32768]{1,0:T(8,128)(2,1)}, bf16[16,32768]{1,0:T(8,128)(2,1)S(1)}, u32[]{:S(2)}) copy-start(bf16[16,32768]{1,0:T(8,128)(2,1)S(1)} %fusion.40) | copy-start | bytes 3145732
  109.2 7.1 %collective-permute-start.4 = (bf16[16,8192]{1,0:T(8,128)(2,1)S(1)}, bf16[16,8192]{1,0:T(8,128)(2,1)S(1)}, u32[]{:S(2)}, u32[]{:S(2)}) collective-permute-start(bf16[16,8192]{1,0:T(8,128)(2,1)S(1)} %get-tuple-element.56), channel_id=1, source_target_pairs={{0,4},{4,8},{8,12},{12,16},{16,20},{20,24},{24,28},{28,32},{32,36}... | collective-permute-start | bytes 786440 | tf_op jit(solution)/shard_map/ppermute | solution.py:15
  115.0 5.4 collective-permute-start.5
  129.6 3.0 copy-start.12
  147.0 11.7 %copy-start.8 = (f32[16,128,125]{2,0,1:T(8,128)S(1)}, f32[16,128,125]{2,0,1:T(8,128)}, u32[]{:S(2)}) copy-start(f32[16,128,125]{2,0,1:T(8,128)} %copy.43) | copy-start | bytes 3072004
  147.0 11.7 %copy-start.13 = (s32[125,128]{0,1:T(8,128)S(1)}, s32[125,128]{0,1:T(8,128)}, u32[]{:S(2)}) copy-start(s32[125,128]{0,1:T(8,128)} %copy-done.10) | copy-start | bytes 192004
  147.0 11.7 %copy-start.15 = (f32[125,128]{0,1:T(8,128)S(1)}, f32[125,128]{0,1:T(8,128)}, u32[]{:S(2)}) copy-start(f32[125,128]{0,1:T(8,128)} %copy.21) | copy-start | bytes 192004
  147.0 11.7 %copy-start.18 = (f32[16,125,128]{1,0,2:T(8,128)S(1)}, f32[16,125,128]{1,0,2:T(8,128)}, u32[]{:S(2)}) copy-start(f32[16,125,128]{1,0,2:T(8,128)} %get-tuple-element.81) | copy-start | bytes 3072004
  158.8 9.9 %copy-start.17 = (f32[16,125,128]{1,0,2:T(8,128)S(1)}, f32[16,125,128]{1,0,2:T(8,128)}, u32[]{:S(2)}) copy-start(f32[16,125,128]{1,0,2:T(8,128)} %get-tuple-element.79) | copy-start | bytes 3072004
  168.6 10.1 %copy-start.16 = (f32[16,125,128]{1,0,2:T(8,128)S(1)}, f32[16,125,128]{1,0,2:T(8,128)}, u32[]{:S(2)}) copy-start(f32[16,125,128]{1,0,2:T(8,128)} %get-tuple-element.77) | copy-start | bytes 3072004
  199.4 10.9 %copy-start.3 = (bf16[16,32768]{1,0:T(8,128)(2,1)S(1)}, bf16[16,32768]{1,0:T(8,128)(2,1)}, u32[]{:S(2)}) copy-start(bf16[16,32768]{1,0:T(8,128)(2,1)} %param.12) | copy-start | bytes 3145732
  199.4 10.9 %copy-start.5 = (bf16[16,32768]{1,0:T(8,128)(2,1)S(1)}, bf16[16,32768]{1,0:T(8,128)(2,1)}, u32[]{:S(2)}) copy-start(bf16[16,32768]{1,0:T(8,128)(2,1)} %copy-done.4) | copy-start | bytes 3145732
  199.4 8.9 %collective-permute-start.6 = (bf16[16,8192]{1,0:T(8,128)(2,1)S(1)}, bf16[16,8192]{1,0:T(8,128)(2,1)S(1)}, u32[]{:S(2)}, u32[]{:S(2)}) collective-permute-start(bf16[16,8192]{1,0:T(8,128)(2,1)S(1)} %get-tuple-element.53), channel_id=1, source_target_pairs={{4,0},{8,4},{12,8},{16,12},{20,16},{24,20},{28,24},{32,28},{36,32}... | collective-permute-start | bytes 786440 | tf_op jit(solution)/shard_map/ppermute | solution.py:26
  201.0 8.4 %collective-permute-start.7 = (bf16[16,8192]{1,0:T(8,128)(2,1)S(1)}, bf16[16,8192]{1,0:T(8,128)(2,1)S(1)}, u32[]{:S(2)}, u32[]{:S(2)}) collective-permute-start(bf16[16,8192]{1,0:T(8,128)(2,1)S(1)} %get-tuple-element.52), channel_id=1, source_target_pairs={{0,4},{4,8},{8,12},{12,16},{16,20},{20,24},{24,28},{28,32},{32,36}... | collective-permute-start | bytes 786440 | tf_op jit(solution)/shard_map/ppermute | solution.py:26
Sparse Core Ops, SparseCore 0:
  211.9 75.0 all-gather.1
where the time goes:
time: 572 us; the launch traced here: 567 us
  blocking collectives  251 us (44%)
  matrix products  122 us (21%)
  waiting for transfers between devices  81.5 us (14%)
  local copies, waits for them, and re-layouts  37.1 us (6%)
  other arithmetic  33.2 us (6%)
  starting transfers between devices  27 us (5%)
  between operations  15.2 us (3%)
    psum x1, blocking collectives, per_device(): intersection = lax.psum(partial_intersection, 'node') / total_nodes  251 us
    dot_general x8, matrix products, cell_terms(): jnp.einsum('sjk,jkn->skn', mixed, picker.astype(jnp.float32), precision=l...  82.7 us
    all_gather x1, waiting for transfers between devices, per_device(): panel = lax.all_gather(second, 'state', axis=0, tiled=True)  75.3 us
    dot_general x8, matrix products, cell_terms(): jnp.einsum('skn,jkn->sjk', part_pair, picker_half, preferred_element_type...  27.9 us
    ppermute x4, starting transfers between devices, passed_along(): return lax.ppermute(block, axis, route)  16.9 us
  transfers between devices with their start and end apart: 9, of which 4 were waited for; matrix products, arithmetic and copies ran while one was open for 1% of the time, Pallas kernels for 0%

commit v1 on v0

--- a/solution.py
+++ b/solution.py
@@ -5,6 +5,19 @@
 
 CENTER = 3.0
 HALF_WIDTH = 3.0
+
+
+def ring_gather(x, axis, dim):
+    ways = lax.axis_size(axis)
+    up = [(d, (d + 1) % ways) for d in range(ways)]
+    down = [(d, (d - 1) % ways) for d in range(ways)]
+    earlier, later = ([x], [x])
+    for _ in range(ways // 2):
+        earlier.append(lax.ppermute(earlier[-1], axis, up))
+    for _ in range((ways - 1) // 2):
+        later.append(lax.ppermute(later[-1], axis, down))
+    line = jnp.concatenate([*earlier[::-1], *later[1:]], axis=dim)
+    return jnp.roll(line, (lax.axis_index(axis) - ways // 2) * x.shape[dim], axis=dim)
 
 
 def extended(block, sides, width):
@@ -101,7 +114,7 @@
         jnp.bfloat16
     )
     total_nodes = block.shape[1] * lax.axis_size("node")
-    panel = lax.all_gather(second, "state", axis=0, tiled=True)
+    panel = ring_gather(second, "state", 0)
     partial_intersection = jnp.einsum("an,bn->ab", panel, panel, preferred_element_type=jnp.float32)
     intersection = lax.psum(partial_intersection, "node") / total_nodes
     factor, inverse = factorize(intersection)

time: 572 us -> 546 us (0.955)
  the two profiles are of different devices: /device:TPU:2 before, /device:TPU:128 now
where the time goes in v1:
time: 546 us; the launch traced here: 541 us
  blocking collectives  247 us (45%)
  matrix products  118 us (22%)
  waiting for transfers between devices  58.3 us (11%)
  local copies, waits for them, and re-layouts  42.9 us (8%)
  starting transfers between devices  40.7 us (7%)
  other arithmetic  32.2 us (6%)
    psum x1, blocking collectives, per_device(): intersection = lax.psum(partial_intersection, 'node') / total_nodes  247 us
    dot_general x8, matrix products, cell_terms(): jnp.einsum('sjk,jkn->skn', mixed, picker.astype(jnp.float32), precision=l...  82.7 us
    ppermute x2, waiting for transfers between devices, ring_gather(): earlier.append(lax.ppermute(earlier[-1], axis, up))  36.4 us
    dot_general x8, matrix products, cell_terms(): jnp.einsum('skn,jkn->sjk', part_pair, picker_half, preferred_element_type...  27.9 us
    ppermute x4, starting transfers between devices, passed_along(): return lax.ppermute(block, axis, route)  18.2 us
    ppermute x4, waiting for transfers between devices, passed_along(): return lax.ppermute(block, axis, route)  18 us
    ppermute x2, starting transfers between devices, extended(): lax.ppermute(lax.slice_in_dim(block, 0, width, axis=dim), axis, backward)  13.9 us
  transfers between devices with their start and end apart: 11, of which 8 were waited for; matrix products, arithmetic and copies ran while one was open for 1% of the time, Pallas kernels for 0%

profile of v1, /device:TPU:128, one launch (start us, length us, event | category | flops | bytes accessed | tf_op | source)
XLA Modules:
  0.0 541.0 jit_solution(15764987307008870255)
XLA Ops:
  1.8 1.9 collective-permute-start
  3.7 7.0 %collective-permute-start.1 = (bf16[16,8192]{1,0:T(8,128)(2,1)S(1)}, bf16[16,8192]{1,0:T(8,128)(2,1)S(1)}, u32[]{:S(2)}, u32[]{:S(2)}) collective-permute-start(bf16[16,8192]{1,0:T(8,128)(2,1)S(1)} %get-tuple-element.59), channel_id=1, source_target_pairs={{4,0},{8,4},{12,8},{16,12},{20,16},{24,20},{28,24},{32,28},{36,32}... | collective-permute-start | bytes 786440 | tf_op jit(solution)/shard_map/ppermute | solution.py:31
  16.1 3.2 reshape.132
  21.0 2.8 fusion.34
  23.8 2.0 copy-done.6
  25.8 3.0 fusion.127
  29.7 4.3 fusion.126
  34.8 4.3 fusion.125
  41.0 4.2 fusion.124
  47.0 11.6 %fusion.45 = f32[16,128,192]{2,0,1:T(8,128)S(1)} fusion(s32[125,128]{0,1:T(8,128)S(1)} %copy.16, f32[16,128,125]{2,0,1:T(8,128)S(1)} %copy.33, f32[16,125,128]{1,0,2:T(8,128)} %get-tuple-element.75, f32[125,128]{0,1:T(8,128)} %copy.19), kind=kOutput, calls=%fused_computation.62 | convolution fusion | flops 593408000 | bytes 3748864 | tf_op jit(solution)/shard_map/sjk,jkn->skn/dot_general | solution.py:71
  58.6 9.9 %fusion.47 = f32[16,128,192]{2,0,1:T(8,128)S(1)} fusion(s32[125,128]{0,1:T(8,128)S(1)} %copy-done.12, f32[16,128,125]{2,0,1:T(8,128)S(1)} %copy.35, f32[16,125,128]{1,0,2:T(8,128)S(1)} %copy-done.20, f32[125,128]{0,1:T(8,128)S(1)} %copy-done.15), kind=kOutput, calls=%fused_computation.64 | convolution fusion | flops 593408000 | bytes 3748864 | tf_op jit(solution)/shard_map/sjk,jkn->skn/dot_general | solution.py:71
  68.5 10.0 %fusion.49 = f32[16,128,192]{2,0,1:T(8,128)S(1)} fusion(s32[125,128]{0,1:T(8,128)S(1)} %copy.22, f32[16,128,125]{2,0,1:T(8,128)S(1)} %copy-done.8, f32[16,125,128]{1,0,2:T(8,128)S(1)} %copy-done.21, f32[125,128]{0,1:T(8,128)S(1)} %copy.23), kind=kOutput, calls=%fused_computation.66 | convolution fusion | flops 593408000 | bytes 3748864 | tf_op jit(solution)/shard_map/sjk,jkn->skn/dot_general | solution.py:71
  78.5 9.8 %fusion.51 = f32[16,128,192]{2,0,1:T(8,128)S(1)} fusion(s32[125,128]{0,1:T(8,128)S(1)} %copy.24, f32[16,128,125]{2,0,1:T(8,128)S(1)} %copy-done.10, f32[16,125,128]{1,0,2:T(8,128)S(1)} %copy-done.22, f32[125,128]{0,1:T(8,128)S(1)} %copy.25), kind=kOutput, calls=%fused_computation.68 | convolution fusion | flops 593408000 | bytes 3748864 | tf_op jit(solution)/shard_map/sjk,jkn->skn/dot_general | solution.py:71
  89.4 2.3 fusion.37
  91.7 3.3 copy.26
  94.9 4.0 reshape.133
  99.2 7.1 %collective-permute-start.2 = (bf16[16,8192]{1,0:T(8,128)(2,1)S(1)}, bf16[16,8192]{1,0:T(8,128)(2,1)S(1)}, u32[]{:S(2)}, u32[]{:S(2)}) collective-permute-start(bf16[16,8192]{1,0:T(8,128)(2,1)S(1)} %get-tuple-element.55), channel_id=1, source_target_pairs={{4,0},{8,4},{12,8},{16,12},{20,16},{24,20},{28,24},{32,28},{36,32}... | collective-permute-start | bytes 786440 | tf_op jit(solution)/shard_map/ppermute | solution.py:39
  107.0 1.9 collective-permute-start.3
  110.2 7.9 %collective-permute-done.3 = bf16[16,8192]{1,0:T(8,128)(2,1)S(1)} collective-permute-done((bf16[16,8192]{1,0:T(8,128)(2,1)S(1)}, bf16[16,8192]{1,0:T(8,128)(2,1)S(1)}, u32[]{:S(2)}, u32[]{:S(2)}) %collective-permute-start.3) | collective-permute-done | bytes 262176 | tf_op jit(solution)/shard_map/ppermute | solution.py:39
  119.2 1.9 collective-permute-start.4
  121.2 7.0 %collective-permute-start.5 = (bf16[16,8192]{1,0:T(8,128)(2,1)S(1)}, bf16[16,8192]{1,0:T(8,128)(2,1)S(1)}, u32[]{:S(2)}, u32[]{:S(2)}) collective-permute-start(bf16[16,8192]{1,0:T(8,128)(2,1)S(1)} %get-tuple-element.57), channel_id=1, source_target_pairs={{4,0},{8,4},{12,8},{16,12},{20,16},{24,20},{28,24},{32,28},{36,32}... | collective-permute-start | bytes 786440 | tf_op jit(solution)/shard_map/ppermute | solution.py:31
  128.1 2.1 collective-permute-done.4
  130.2 1.8 collective-permute-done.5
  133.3 3.2 reshape.134
  138.2 3.0 fusion.35
  141.2 3.0 fusion.131
  144.3 3.0 fusion.130
  147.3 3.0 fusion.129
  150.3 3.0 fusion.128
  158.7 11.7 %fusion.46 = f32[16,128,192]{2,0,1:T(8,128)S(1)} fusion(s32[125,128]{0,1:T(8,128)S(1)} %copy.16, f32[16,128,125]{2,0,1:T(8,128)} %copy.41, f32[16,125,128]{1,0,2:T(8,128)} %get-tuple-element.83, f32[125,128]{0,1:T(8,128)} %copy.19), kind=kOutput, calls=%fused_computation.63 | convolution fusion | flops 593408000 | bytes 3748864 | tf_op jit(solution)/shard_map/sjk,jkn->skn/dot_general | solution.py:71
  170.4 9.9 %fusion.48 = f32[16,128,192]{2,0,1:T(8,128)S(1)} fusion(s32[125,128]{0,1:T(8,128)S(1)} %copy-done.14, f32[16,128,125]{2,0,1:T(8,128)S(1)} %copy-done.9, f32[16,125,128]{1,0,2:T(8,128)S(1)} %copy-done.19, f32[125,128]{0,1:T(8,128)S(1)} %copy-done.16), kind=kOutput, calls=%fused_computation.65 | convolution fusion | flops 593408000 | bytes 3748864 | tf_op jit(solution)/shard_map/sjk,jkn->skn/dot_general | solution.py:71
  180.3 10.0 %fusion.50 = f32[16,128,192]{2,0,1:T(8,128)S(1)} fusion(s32[125,128]{0,1:T(8,128)S(1)} %copy.22, f32[16,128,125]{2,0,1:T(8,128)S(1)} %copy.45, f32[16,125,128]{1,0,2:T(8,128)S(1)} %copy-done.18, f32[125,128]{0,1:T(8,128)S(1)} %copy.23), kind=kOutput, calls=%fused_computation.67 | convolution fusion | flops 593408000 | bytes 3748864 | tf_op jit(solution)/shard_map/sjk,jkn->skn/dot_general | solution.py:71
  190.3 9.8 %fusion.52 = f32[16,128,192]{2,0,1:T(8,128)S(1)} fusion(s32[125,128]{0,1:T(8,128)S(1)} %copy.24, f32[16,128,125]{2,0,1:T(8,128)S(1)} %copy.47, f32[16,125,128]{1,0,2:T(8,128)S(1)} %copy-done.17, f32[125,128]{0,1:T(8,128)S(1)} %copy.25), kind=kOutput, calls=%fused_computation.69 | convolution fusion | flops 593408000 | bytes 3748864 | tf_op jit(solution)/shard_map/sjk,jkn->skn/dot_general | solution.py:71
  201.2 2.3 fusion.36
  203.6 3.3 copy.29
  206.8 4.0 reshape.135
  211.1 7.3 %collective-permute-start.6 = (bf16[16,8192]{1,0:T(8,128)(2,1)S(1)}, bf16[16,8192]{1,0:T(8,128)(2,1)S(1)}, u32[]{:S(2)}, u32[]{:S(2)}) collective-permute-start(bf16[16,8192]{1,0:T(8,128)(2,1)S(1)} %get-tuple-element.53), channel_id=1, source_target_pairs={{4,0},{8,4},{12,8},{16,12},{20,16},{24,20},{28,24},{32,28},{36,32}... | collective-permute-start | bytes 786440 | tf_op jit(solution)/shard_map/ppermute | solution.py:39
  218.5 1.9 collective-permute-start.7
  220.4 1.8 collective-permute-done.6
  222.3 7.2 %collective-permute-done.7 = bf16[16,8192]{1,0:T(8,128)(2,1)S(1)} collective-permute-done((bf16[16,8192]{1,0:T(8,128)(2,1)S(1)}, bf16[16,8192]{1,0:T(8,128)(2,1)S(1)}, u32[]{:S(2)}, u32[]{:S(2)}) %collective-permute-start.7) | collective-permute-done | bytes 262176 | tf_op jit(solution)/shard_map/ppermute | solution.py:39
  232.4 21.8 %collective-permute-done.8 = bf16[16,32768]{1,0:T(8,128)(2,1)S(1)} collective-permute-done((bf16[16,32768]{1,0:T(8,128)(2,1)S(1)}, bf16[16,32768]{1,0:T(8,128)(2,1)S(1)}, u32[]{:S(2)}, u32[]{:S(2)}) %collective-permute-start.8) | collective-permute-done | bytes 1048608 | tf_op jit(solution)/shard_map/ppermute | solution.py:16
  255.7 1.7 collective-permute-start.10
  257.4 14.6 %collective-permute-done.9 = bf16[16,32768]{1,0:T(8,128)(2,1)S(1)} collective-permute-done((bf16[16,32768]{1,0:T(8,128)(2,1)S(1)}, bf16[16,32768]{1,0:T(8,128)(2,1)S(1)}, u32[]{:S(2)}, u32[]{:S(2)}) %collective-permute-start.9) | collective-permute-done | bytes 1048608 | tf_op jit(solution)/shard_map/ppermute | solution.py:16
  272.7 3.3 copy-done.7
  277.2 246.6 %psum.7 = f32[64,64]{0,1:T(8,128)S(1)} all-reduce(f32[64,64]{0,1:T(8,128)S(1)} %fusion.39), channel_id=1, replica_groups=mesh['node'=64,'state'=4] {'node'}, use_global_device_ids=true, to_apply=%region_1.0 | all-reduce | flops 4096 | bytes 32768 | tf_op jit(solution)/shard_map/psum | solution.py:119
  523.8 5.8 %cholesky.17 = f32[64,64]{1,0:T(8,128)S(1)} custom-call(f32[64,64]{1,0:T(8,128)S(1)} %fusion.107), custom_call_target="Cholesky" | custom-call | tf_op jit(solution)/shard_map/jit(cholesky)/cholesky | solution.py:100
  531.6 4.9 custom-call.6
  536.8 3.8 convolution_convert_fusion
  (117 shorter events, 36.1 us)
Async XLA Ops:
  0.6 28.2 %copy-start = (bf16[125,125]{1,0:T(8,128)(2,1)S(1)}, bf16[125,125]{1,0:T(8,128)(2,1)}, u32[]{:S(2)}) copy-start(bf16[125,125]{1,0:T(8,128)(2,1)} %param.15) | copy-start | bytes 93754
  0.6 14.1 %copy-start.1 = (bf16[16,32768]{1,0:T(8,128)(2,1)S(1)}, bf16[16,32768]{1,0:T(8,128)(2,1)}, u32[]{:S(2)}) copy-start(bf16[16,32768]{1,0:T(8,128)(2,1)} %param.12) | copy-start | bytes 3145732
  1.8 12.9 %collective-permute-start = (bf16[16,8192]{1,0:T(8,128)(2,1)S(1)}, bf16[16,8192]{1,0:T(8,128)(2,1)S(1)}, u32[]{:S(2)}, u32[]{:S(2)}) collective-permute-start(bf16[16,8192]{1,0:T(8,128)(2,1)S(1)} %get-tuple-element.58), channel_id=1, source_target_pairs={{0,4},{4,8},{8,12},{12,16},{16,20},{20,24},{24,28},{28,32},{32,36}... | collective-permute-start | bytes 786440 | tf_op jit(solution)/shard_map/ppermute | solution.py:28
  3.7 11.0 %collective-permute-start.1 = (bf16[16,8192]{1,0:T(8,128)(2,1)S(1)}, bf16[16,8192]{1,0:T(8,128)(2,1)S(1)}, u32[]{:S(2)}, u32[]{:S(2)}) collective-permute-start(bf16[16,8192]{1,0:T(8,128)(2,1)S(1)} %get-tuple-element.59), channel_id=1, source_target_pairs={{4,0},{8,4},{12,8},{16,12},{20,16},{24,20},{28,24},{32,28},{36,32}... | collective-permute-start | bytes 786440 | tf_op jit(solution)/shard_map/ppermute | solution.py:31
  13.6 16.0 %copy-start.11 = (s32[125,128]{0,1:T(8,128)}, s32[125,128]{0,1:T(8,128)S(1)}, u32[]{:S(2)}) copy-start(s32[125,128]{0,1:T(8,128)S(1)} %copy.20) | copy-start | bytes 192004
  23.8 2.0 copy-start.6
  47.0 11.6 %copy-start.12 = (s32[125,128]{0,1:T(8,128)S(1)}, s32[125,128]{0,1:T(8,128)}, u32[]{:S(2)}) copy-start(s32[125,128]{0,1:T(8,128)} %copy-done.11) | copy-start | bytes 192004
  47.0 11.6 %copy-start.15 = (f32[125,128]{0,1:T(8,128)S(1)}, f32[125,128]{0,1:T(8,128)}, u32[]{:S(2)}) copy-start(f32[125,128]{0,1:T(8,128)} %copy.21) | copy-start | bytes 192004
  47.0 11.6 %copy-start.20 = (f32[16,125,128]{1,0,2:T(8,128)S(1)}, f32[16,125,128]{1,0,2:T(8,128)}, u32[]{:S(2)}) copy-start(f32[16,125,128]{1,0,2:T(8,128)} %get-tuple-element.73) | copy-start | bytes 3072004
  58.5 9.9 %copy-start.8 = (f32[16,128,125]{2,0,1:T(8,128)S(1)}, f32[16,128,125]{2,0,1:T(8,128)}, u32[]{:S(2)}) copy-start(f32[16,128,125]{2,0,1:T(8,128)} %copy.37) | copy-start | bytes 3072004
  58.5 9.9 %copy-start.21 = (f32[16,125,128]{1,0,2:T(8,128)S(1)}, f32[16,125,128]{1,0,2:T(8,128)}, u32[]{:S(2)}) copy-start(f32[16,125,128]{1,0,2:T(8,128)} %get-tuple-element.71) | copy-start | bytes 3072004
  68.4 10.0 %copy-start.10 = (f32[16,128,125]{2,0,1:T(8,128)S(1)}, f32[16,128,125]{2,0,1:T(8,128)}, u32[]{:S(2)}) copy-start(f32[16,128,125]{2,0,1:T(8,128)} %copy.39) | copy-start | bytes 3072004
  68.4 10.1 %copy-start.22 = (f32[16,125,128]{1,0,2:T(8,128)S(1)}, f32[16,125,128]{1,0,2:T(8,128)}, u32[]{:S(2)}) copy-start(f32[16,125,128]{1,0,2:T(8,128)} %get-tuple-element.69) | copy-start | bytes 3072004
  99.1 19.7 %copy-start.2 = (bf16[16,32768]{1,0:T(8,128)(2,1)S(1)}, bf16[16,32768]{1,0:T(8,128)(2,1)}, u32[]{:S(2)}) copy-start(bf16[16,32768]{1,0:T(8,128)(2,1)} %param.12) | copy-start | bytes 3145732
  99.2 10.9 %collective-permute-start.2 = (bf16[16,8192]{1,0:T(8,128)(2,1)S(1)}, bf16[16,8192]{1,0:T(8,128)(2,1)S(1)}, u32[]{:S(2)}, u32[]{:S(2)}) collective-permute-start(bf16[16,8192]{1,0:T(8,128)(2,1)S(1)} %get-tuple-element.55), channel_id=1, source_target_pairs={{4,0},{8,4},{12,8},{16,12},{20,16},{24,20},{28,24},{32,28},{36,32}... | collective-permute-start | bytes 786440 | tf_op jit(solution)/shard_map/ppermute | solution.py:39
  107.0 11.0 %collective-permute-start.3 = (bf16[16,8192]{1,0:T(8,128)(2,1)S(1)}, bf16[16,8192]{1,0:T(8,128)(2,1)S(1)}, u32[]{:S(2)}, u32[]{:S(2)}) collective-permute-start(bf16[16,8192]{1,0:T(8,128)(2,1)S(1)} %get-tuple-element.54), channel_id=1, source_target_pairs={{0,4},{4,8},{8,12},{12,16},{16,20},{20,24},{24,28},{28,32},{32,36}... | collective-permute-start | bytes 786440 | tf_op jit(solution)/shard_map/ppermute | solution.py:39
  119.2 12.8 %copy-start.4 = (bf16[16,32768]{1,0:T(8,128)(2,1)}, bf16[16,32768]{1,0:T(8,128)(2,1)S(1)}, u32[]{:S(2)}) copy-start(bf16[16,32768]{1,0:T(8,128)(2,1)S(1)} %fusion.43) | copy-start | bytes 3145732
  119.2 11.0 %collective-permute-start.4 = (bf16[16,8192]{1,0:T(8,128)(2,1)S(1)}, bf16[16,8192]{1,0:T(8,128)(2,1)S(1)}, u32[]{:S(2)}, u32[]{:S(2)}) collective-permute-start(bf16[16,8192]{1,0:T(8,128)(2,1)S(1)} %get-tuple-element.56), channel_id=1, source_target_pairs={{0,4},{4,8},{8,12},{12,16},{16,20},{20,24},{24,28},{28,32},{32,36}... | collective-permute-start | bytes 786440 | tf_op jit(solution)/shard_map/ppermute | solution.py:28
  121.2 10.8 %collective-permute-start.5 = (bf16[16,8192]{1,0:T(8,128)(2,1)S(1)}, bf16[16,8192]{1,0:T(8,128)(2,1)S(1)}, u32[]{:S(2)}, u32[]{:S(2)}) collective-permute-start(bf16[16,8192]{1,0:T(8,128)(2,1)S(1)} %get-tuple-element.57), channel_id=1, source_target_pairs={{4,0},{8,4},{12,8},{16,12},{20,16},{24,20},{28,24},{32,28},{36,32}... | collective-permute-start | bytes 786440 | tf_op jit(solution)/shard_map/ppermute | solution.py:31
  141.2 3.1 copy-start.13
  158.6 11.8 %copy-start.9 = (f32[16,128,125]{2,0,1:T(8,128)S(1)}, f32[16,128,125]{2,0,1:T(8,128)}, u32[]{:S(2)}) copy-start(f32[16,128,125]{2,0,1:T(8,128)} %copy.43) | copy-start | bytes 3072004
  158.6 11.8 %copy-start.14 = (s32[125,128]{0,1:T(8,128)S(1)}, s32[125,128]{0,1:T(8,128)}, u32[]{:S(2)}) copy-start(s32[125,128]{0,1:T(8,128)} %copy-done.11) | copy-start | bytes 192004
  158.6 11.8 %copy-start.16 = (f32[125,128]{0,1:T(8,128)S(1)}, f32[125,128]{0,1:T(8,128)}, u32[]{:S(2)}) copy-start(f32[125,128]{0,1:T(8,128)} %copy.21) | copy-start | bytes 192004
  158.6 11.8 %copy-start.19 = (f32[16,125,128]{1,0,2:T(8,128)S(1)}, f32[16,125,128]{1,0,2:T(8,128)}, u32[]{:S(2)}) copy-start(f32[16,125,128]{1,0,2:T(8,128)} %get-tuple-element.81) | copy-start | bytes 3072004
  170.4 9.9 %copy-start.18 = (f32[16,125,128]{1,0,2:T(8,128)S(1)}, f32[16,125,128]{1,0,2:T(8,128)}, u32[]{:S(2)}) copy-start(f32[16,125,128]{1,0,2:T(8,128)} %get-tuple-element.79) | copy-start | bytes 3072004
  180.3 10.1 %copy-start.17 = (f32[16,125,128]{1,0,2:T(8,128)S(1)}, f32[16,125,128]{1,0,2:T(8,128)}, u32[]{:S(2)}) copy-start(f32[16,125,128]{1,0,2:T(8,128)} %get-tuple-element.77) | copy-start | bytes 3072004
  211.0 19.3 %copy-start.3 = (bf16[16,32768]{1,0:T(8,128)(2,1)S(1)}, bf16[16,32768]{1,0:T(8,128)(2,1)}, u32[]{:S(2)}) copy-start(bf16[16,32768]{1,0:T(8,128)(2,1)} %param.12) | copy-start | bytes 3145732
  211.0 19.3 %copy-start.5 = (bf16[16,32768]{1,0:T(8,128)(2,1)S(1)}, bf16[16,32768]{1,0:T(8,128)(2,1)}, u32[]{:S(2)}) copy-start(bf16[16,32768]{1,0:T(8,128)(2,1)} %copy-done.4) | copy-start | bytes 3145732
  211.1 11.1 %collective-permute-start.6 = (bf16[16,8192]{1,0:T(8,128)(2,1)S(1)}, bf16[16,8192]{1,0:T(8,128)(2,1)S(1)}, u32[]{:S(2)}, u32[]{:S(2)}) collective-permute-start(bf16[16,8192]{1,0:T(8,128)(2,1)S(1)} %get-tuple-element.53), channel_id=1, source_target_pairs={{4,0},{8,4},{12,8},{16,12},{20,16},{24,20},{28,24},{32,28},{36,32}... | collective-permute-start | bytes 786440 | tf_op jit(solution)/shard_map/ppermute | solution.py:39
  218.5 11.0 %collective-permute-start.7 = (bf16[16,8192]{1,0:T(8,128)(2,1)S(1)}, bf16[16,8192]{1,0:T(8,128)(2,1)S(1)}, u32[]{:S(2)}, u32[]{:S(2)}) collective-permute-start(bf16[16,8192]{1,0:T(8,128)(2,1)S(1)} %get-tuple-element.52), channel_id=1, source_target_pairs={{0,4},{4,8},{8,12},{12,16},{16,20},{20,24},{24,28},{28,32},{32,36}... | collective-permute-start | bytes 786440 | tf_op jit(solution)/shard_map/ppermute | solution.py:39
  230.8 23.4 %collective-permute-start.8 = (bf16[16,32768]{1,0:T(8,128)(2,1)S(1)}, bf16[16,32768]{1,0:T(8,128)(2,1)S(1)}, u32[]{:S(2)}, u32[]{:S(2)}) collective-permute-start(bf16[16,32768]{1,0:T(8,128)(2,1)S(1)} %fusion.44), channel_id=1, source_target_pairs={{0,1},{1,2},{2,3},{3,0},{4,5},{5,6},{6,7},{7,4},{8,9},{9,10},{10,1... | collective-permute-start | bytes 3145736 | tf_op jit(solution)/shard_map/ppermute | solution.py:16
  254.2 17.9 %collective-permute-start.9 = (bf16[16,32768]{1,0:T(8,128)(2,1)S(1)}, bf16[16,32768]{1,0:T(8,128)(2,1)S(1)}, u32[]{:S(2)}, u32[]{:S(2)}) collective-permute-start(bf16[16,32768]{1,0:T(8,128)(2,1)S(1)} %collective-permute-done.8), channel_id=1, source_target_pairs={{0,1},{1,2},{2,3},{3,0},{4,5},{5,6},{6,7},{7,4},{8,9},{9,10},{10,1... | collective-permute-start | bytes 3145736 | tf_op jit(solution)/shard_map/ppermute | solution.py:16
  255.7 16.6 %collective-permute-start.10 = (bf16[16,32768]{1,0:T(8,128)(2,1)S(1)}, bf16[16,32768]{1,0:T(8,128)(2,1)S(1)}, u32[]{:S(2)}, u32[]{:S(2)}) collective-permute-start(bf16[16,32768]{1,0:T(8,128)(2,1)S(1)} %fusion.44), channel_id=1, source_target_pairs={{0,3},{1,0},{2,1},{3,2},{4,7},{5,4},{6,5},{7,6},{8,11},{9,8},{10,9... | collective-permute-start | bytes 3145736 | tf_op jit(solution)/shard_map/ppermute | solution.py:18
  272.6 3.3 copy-start.7
